TPU v7x, 32 devices: a whole 2x2x4 slice. The times are simulated.
32 devices in a mesh: seq: 8 (over z, y), head: 4 (over x, core).
Axes of the slice: x: 2, y: 2, z: 4, core: 2. Of those that a mesh axis runs over, the one named last changes fastest.
Arguments:
- query: bfloat16 [4096, 1024], P('seq', 'head'), may hold values from -70 to 70
- key: bfloat16 [4096, 1024], P('seq', 'head'), may hold values from -15 to 15
- value: bfloat16 [4096, 1024], P('seq', 'head'), may hold values from -6 to 6
- middle_offsets: int32 [16], P('head'), may hold values from 0 to 3
- upper_offsets: int32 [16], P('head'), may hold values from 0 to 3
- out_weight: bfloat16 [1024, 1024], P('head'), may hold values from -0.1875 to 0.1875
Outputs:
- projected: bfloat16 [4096, 1024], P(('seq', 'head'))
All inputs are finite; a program needn't handle non-finite values.
Results may differ from a plain program's by a relative error of at most 0.0051.
Values may be sent and summed in bfloat16 or wider, within the bound.
A program may use at most 64 MiB of HBM per device.

v0:
```python
import jax
import jax.numpy as jnp
from jax import lax
from jax.sharding import PartitionSpec as P

HD = 64
SPAN = 8
MIDDLE_DILATION = 4


def partner_2(value, axis, stride):
    mask = 2**stride
    pairs = [(source, source ^ mask) for source in range(lax.axis_size(axis))]
    return lax.ppermute(value, axis, pairs)


def attend_segment(query_matrix_rows, key_matrix_rows, value_matrix_rows):
    scores = jnp.einsum(
        "qhd,khd->hqk", query_matrix_rows, key_matrix_rows, preferred_element_type=jnp.float32
    ) * HD ** (-0.5)
    row_max = jnp.max(scores, axis=2)
    mass = jnp.exp(scores - row_max[:, :, None])
    total = jnp.sum(mass, axis=2)
    soft_weights = mass.astype(jnp.bfloat16)
    weighted = jnp.einsum(
        "hqk,khd->qhd", soft_weights, value_matrix_rows, preferred_element_type=jnp.float32
    )
    return (weighted, total.T, row_max.T)


def attend_blocks(query_matrix_rows, key_matrix_rows, value_matrix_rows):
    block_size = min(512, query_matrix_rows.shape[0])
    pieces = query_matrix_rows.reshape(
        query_matrix_rows.shape[0] // block_size,
        block_size,
        query_matrix_rows.shape[1],
        query_matrix_rows.shape[2],
    )

    def one_block(one_piece):
        return attend_segment(one_piece, key_matrix_rows, value_matrix_rows)

    weighted, total, row_max = lax.map(one_block, pieces)
    return (
        weighted.reshape(query_matrix_rows.shape),
        total.reshape(query_matrix_rows.shape[:2]),
        row_max.reshape(query_matrix_rows.shape[:2]),
    )


def picked_rows(block_rows, offsets, stride):
    group_count = block_rows.shape[0] // stride
    grouped = block_rows.reshape(group_count, stride, block_rows.shape[1], block_rows.shape[2])
    chosen = (
        jnp.arange(stride, dtype=jnp.int32)[None, :, None, None] == offsets[None, None, :, None]
    )
    return jnp.sum(jnp.where(chosen, grouped, jnp.zeros((), grouped.dtype)), axis=1)


def scatter_rows(values, offsets, stride, filler):
    chosen = jnp.arange(stride, dtype=jnp.int32)[:, None] == offsets[None, :]
    spread_out = jnp.where(chosen[None], values[:, None], filler)
    return spread_out.reshape((values.shape[0] * stride,) + values.shape[1:])


def flatten_level(result):
    row_total = result[0].shape[0]
    weighted = result[0].reshape(row_total, -1)
    total = jnp.repeat(result[1], HD, axis=1)
    row_max = jnp.repeat(result[2], HD, axis=1)
    return (weighted, total, row_max)


def scatter_level(result, offsets, stride):
    weighted, total, row_max = flatten_level(result)
    column_offsets = jnp.repeat(offsets, HD)
    return (
        scatter_rows(weighted, column_offsets, stride, 0.0),
        scatter_rows(total, column_offsets, stride, 0.0),
        scatter_rows(row_max, column_offsets, stride, -jnp.inf),
    )


def combine(levels):
    highest = levels[0][2]
    for one_level in levels[1:]:
        highest = jnp.maximum(highest, one_level[2])
    numerator = jnp.zeros(levels[0][0].shape, jnp.float32)
    denominator = jnp.zeros(levels[0][1].shape, jnp.float32)
    for one_level in levels:
        factor = jnp.exp(one_level[2] - highest)
        numerator = numerator + factor * one_level[0]
        denominator = denominator + factor * one_level[1]
    return (numerator / denominator).astype(jnp.bfloat16)


def per_device(query, key, value, middle_offsets, upper_offsets, out_weight):
    row_count = query.shape[0]
    head_count = query.shape[1] // HD
    top_stride = lax.axis_size("seq") // 2
    query_matrix_rows = query.reshape(row_count, head_count, HD)
    key_matrix_rows = key.reshape(row_count, head_count, HD)
    value_matrix_rows = value.reshape(row_count, head_count, HD)
    top_key_local = picked_rows(key_matrix_rows, upper_offsets, top_stride).reshape(
        -1, head_count * HD
    )
    top_value_local = picked_rows(value_matrix_rows, upper_offsets, top_stride).reshape(
        -1, head_count * HD
    )
    top_key_all, top_value_all = (
        lax.all_gather(top_key_local, "seq", axis=0, tiled=True),
        lax.all_gather(top_value_local, "seq", axis=0, tiled=True),
    )
    upper_level = attend_segment(
        picked_rows(query_matrix_rows, upper_offsets, top_stride),
        top_key_all.reshape(-1, head_count, HD),
        top_value_all.reshape(-1, head_count, HD),
    )
    middle_pair = jnp.stack(
        [
            picked_rows(key_matrix_rows, middle_offsets, MIDDLE_DILATION),
            picked_rows(value_matrix_rows, middle_offsets, MIDDLE_DILATION),
        ]
    ).reshape(2, -1, head_count * HD)
    for bit_number in range(SPAN.bit_length() - 1):
        partner = partner_2(middle_pair, "seq", bit_number)
        middle_pair = jnp.concatenate([middle_pair, partner], axis=1)
    middle_level = attend_segment(
        picked_rows(query_matrix_rows, middle_offsets, MIDDLE_DILATION),
        middle_pair[0].reshape(-1, head_count, HD),
        middle_pair[1].reshape(-1, head_count, HD),
    )
    bottom = flatten_level(attend_blocks(query_matrix_rows, key_matrix_rows, value_matrix_rows))
    attention = combine(
        (
            bottom,
            scatter_level(middle_level, middle_offsets, MIDDLE_DILATION),
            scatter_level(upper_level, upper_offsets, top_stride),
        )
    )
    summed = lax.psum_scatter(
        jnp.dot(attention, out_weight, preferred_element_type=jnp.float32),
        "head",
        scatter_dimension=0,
        tiled=True,
    )
    return summed.astype(jnp.bfloat16)


def solution(mesh):
    in_specs = (
        P("seq", "head"),
        P("seq", "head"),
        P("seq", "head"),
        P("head"),
        P("head"),
        P("head", None),
    )
    out_specs = P(("seq", "head"), None)
    return jax.shard_map(
        per_device, mesh=mesh, in_specs=in_specs, out_specs=out_specs, check_vma=False
    )
```

profile of v0, /device:TPU:0, one launch (start us, length us, event | category | flops | bytes accessed | tf_op | source)
XLA Modules:
  0.0 164.0 jit_solution(4376389824751921904)
XLA Ops:
  6.5 1.3 reshape_reshape.16
  7.8 1.2 reshape_reshape.17
  9.1 1.3 reshape_reshape.18
  10.4 2.6 %select_reduce_fusion.4 = (bf16[128,4,64]{2,1,0:T(4,128)(2,1)S(1)}, bf16[128,4,64]{2,1,0:T(4,128)(2,1)S(1)}, bf16[128,4,64]{2,1,0:T(4,128)(2,1)S(1)}, bf16[128,4...) fusion(bf16[128,4,4,64]{3,2,1,0:T(4,128)(2,1)S(1)} %reshape_reshape.17, ...), kind=kLoop, calls=%fused_computation.41 | loop fusion | flops 1376256 | bytes 1179680 | tf_op jit(solution)/shard_map/reduce_sum | solution.py:57
  13.1 0.1 copy.65
  13.2 0.1 copy.66
  13.4 3.0 %collective-permute-start = (bf16[2,128,256]{1,2,0:T(8,128)(2,1)S(1)}, bf16[2,128,256]{1,2,0:T(8,128)(2,1)S(1)}, u32[]{:S(2)}, u32[]{:S(2)}) collective-permute-start(bf16[2,128,256]{1,2,0:T(8,128)(2,1)S(1)} %pad_maximum_fusion.3), channel_id=1, source_target_pairs={{0,4},{4,0},{8,12},{12,8},{16,20},{20,16},{24,28},{28,24},{1,5},{5... | collective-permute-start | bytes 393224 | tf_op jit(solution)/shard_map/ppermute | solution.py:14
  16.4 0.1 copy.63
  16.5 0.1 copy.64
  16.7 0.1 copy.70
  16.8 28.2 %all_gather.6 = bf16[1024,256]{0,1:T(8,128)(2,1)S(1)} all-gather(bf16[128,256]{0,1:T(8,128)(2,1)S(1)} %bitcast.102), channel_id=1, replica_groups=mesh['seq'=8,'head'=4] {'seq'}, dimensions={0}, use_global_device_ids=true | all-gather | bytes 589824 | tf_op jit(solution)/shard_map/all_gather | solution.py:111
  45.0 0.1 copy.80
  45.1 27.4 %all_gather.7 = bf16[1024,256]{0,1:T(8,128)(2,1)S(1)} all-gather(bf16[128,256]{0,1:T(8,128)(2,1)S(1)} %bitcast.103), channel_id=1, replica_groups=mesh['seq'=8,'head'=4] {'seq'}, dimensions={0}, use_global_device_ids=true | all-gather | bytes 589824 | tf_op jit(solution)/shard_map/all_gather | solution.py:112
  72.6 0.5 multiply_reduce_fusion.1
  73.1 0.5 fusion.8
  73.6 0.6 fusion.10
  74.7 2.7 %multiply_reduce_fusion = (f32[4,512]{1,0:T(4,128)S(1)}, f32[4,512,512]{1,2,0:T(8,128)}) fusion(bf16[512,4,64]{0,2,1:T(8,128)(2,1)S(1)} %bitcast.94, bf16[512,4,64]{0,2,1:T(8,128)(2,1)S(1)} %bitcast.95), kind=kOutput, calls=%fused_computation.1 | convolution fusion | flops 136312832 | bytes 4726784 | tf_op jit(solution)/shard_map/while/body/eval_jaxpr/qhd,khd->hqk/dot_general | solution.py:18
  77.4 0.4 broadcast_select_fusion.4
  77.7 0.6 copy-done.7
  78.3 0.1 copy.74
  78.6 0.2 select_n.70
  78.8 1.0 copy.73
  79.8 0.2 select_n.75
  80.0 1.0 copy.82
  81.0 0.2 select_n.79
  81.2 1.0 copy.86
  82.2 0.5 collective-permute-start.1
  82.7 3.0 %fusion = f32[4,512]{1,0:T(4,128)S(1)} fusion(f32[4,512,512]{1,2,0:T(8,128)} %get-tuple-element.49, f32[4,512]{1,0:T(4,128)S(1)} %get-tuple-element.48), kind=kLoop, calls=%fused_computation.2 | loop fusion | flops 3143680 | bytes 4210688 | tf_op jit(solution)/shard_map/while/body/eval_jaxpr/reduce_sum | solution.py:23
  85.8 8.4 %collective-permute-done.1 = bf16[2,256,256]{1,2,0:T(8,128)(2,1)S(1)} collective-permute-done((bf16[2,256,256]{1,2,0:T(8,128)(2,1)S(1)}, bf16[2,256,256]{1,2,0:T(8,128)(2,1)S(1)}, u32[]{:S(2)}, u32[]{:S(2)}) %collective-permute-start.1) | collective-permute-done | bytes 262176 | tf_op jit(solution)/shard_map/ppermute | solution.py:14
  94.3 0.8 fusion.2
  95.2 13.8 %collective-permute-done.2 = bf16[2,512,256]{1,2,0:T(8,128)(2,1)S(1)} collective-permute-done((bf16[2,512,256]{1,2,0:T(8,128)(2,1)S(1)}, bf16[2,512,256]{1,2,0:T(8,128)(2,1)S(1)}, u32[]{:S(2)}, u32[]{:S(2)}) %collective-permute-start.2) | collective-permute-done | bytes 524320 | tf_op jit(solution)/shard_map/ppermute | solution.py:14
  109.0 0.1 pad_maximum_fusion
  109.1 0.9 fusion.36
  110.0 0.5 multiply_reduce_fusion.2
  110.5 0.5 fusion.6
  111.1 1.6 fusion.12
  112.7 0.1 copy.77
  112.9 1.4 broadcast_select_fusion.5
  114.3 0.2 select_n.66
  114.5 0.2 copy.69
  114.7 2.2 %select_n.72 = f32[512,256]{1,0:T(8,128)} reshape(f32[128,4,256]{2,1,0:T(4,128)} %get-tuple-element.39) | data formatting | bytes 1048576 | tf_op jit(solution)/shard_map/jit(_where)/select_n | solution.py:62
  116.9 2.0 %copy.78 = f32[512,256]{0,1:T(8,128)} copy(f32[512,256]{1,0:T(8,128)} %select_n.72) | data formatting | bytes 1048576 | tf_op jit(solution)/shard_map/jit(_where)/select_n | solution.py:62
  118.9 2.0 %select_n.77 = f32[512,256]{1,0:T(8,128)} reshape(f32[128,4,256]{2,1,0:T(4,128)} %get-tuple-element.40) | data formatting | bytes 1048576 | tf_op jit(solution)/shard_map/jit(_where)/select_n | solution.py:62
  120.9 2.1 %copy.84 = f32[512,256]{0,1:T(8,128)} copy(f32[512,256]{1,0:T(8,128)} %select_n.77) | data formatting | bytes 1048576 | tf_op jit(solution)/shard_map/jit(_where)/select_n | solution.py:62
  123.0 1.6 fusion.28
  124.6 1.8 %fusion.37 = f32[512,1024]{1,0:T(8,128)} fusion(bf16[512,256]{0,1:T(8,128)(2,1)S(1)} %fusion.28, bf16[256,1024]{1,0:T(8,128)(2,1)S(1)} %copy-done), kind=kOutput, calls=%fused_computation.64 | convolution fusion | flops 268435456 | bytes 2883584 | tf_op jit(solution)/shard_map/dot_general | solution.py:142
  126.5 28.9 %reduce-scatter.2.cloned.1.call-done = f32[128,1024]{1,0:T(8,128)} async-done(((f32[512,1024]{1,0:T(8,128)}), f32[128,1024]{1,0:T(8,128)}) %reduce-scatter.2.cloned.1.call-update) | async-done | bytes 524304 | tf_op jit(solution)/shard_map/reduce_scatter | solution.py:141
  155.4 1.8 %convert_element_type.16 = bf16[128,1024]{1,0:T(8,128)(2,1)} convert(f32[128,1024]{1,0:T(8,128)} %reduce-scatter.2.cloned.1.call-done) | non-fusion elementwise | flops 131072 | bytes 786432 | tf_op jit(solution)/shard_map/convert_element_type | solution.py:147
  (42 shorter events, 1.1 us)
Async XLA Ops:
  6.5 118.1 %copy-start = (bf16[256,1024]{1,0:T(8,128)(2,1)S(1)}, bf16[256,1024]{1,0:T(8,128)(2,1)}, u32[]{:S(2)}) copy-start(bf16[256,1024]{1,0:T(8,128)(2,1)} %param.11) | copy-start | bytes 1572868
  6.5 3.9 %copy-start.8 = (s32[4]{0:T(128)S(1)}, s32[4]{0:T(128)}, u32[]{:S(2)}) copy-start(s32[4]{0:T(128)} %param.10) | copy-start | bytes 52
  6.5 3.9 %copy-start.9 = (s32[4]{0:T(128)S(1)}, s32[4]{0:T(128)}, u32[]{:S(2)}) copy-start(s32[4]{0:T(128)} %param.9) | copy-start | bytes 52
  6.5 148.9 %reduce-scatter.2.cloned.1.call-start = ((), (), s32[]{:S(2)}) async-start(), calls=%async_computation.1 | async-start | bytes 2621440 | tf_op jit(solution)/shard_map/reduce_scatter | solution.py:141
  9.1 7.3 %copy-start.5 = (bf16[512,256]{1,0:T(8,128)(2,1)S(1)}, bf16[512,256]{1,0:T(8,128)(2,1)}, u32[]{:S(2)}) copy-start(bf16[512,256]{1,0:T(8,128)(2,1)} %param.6) | copy-start | bytes 786436
  9.1 7.4 %copy-start.6 = (bf16[512,256]{1,0:T(8,128)(2,1)S(1)}, bf16[512,256]{1,0:T(8,128)(2,1)}, u32[]{:S(2)}) copy-start(bf16[512,256]{1,0:T(8,128)(2,1)} %param.7) | copy-start | bytes 786436
  13.4 68.8 %collective-permute-start = (bf16[2,128,256]{1,2,0:T(8,128)(2,1)S(1)}, bf16[2,128,256]{1,2,0:T(8,128)(2,1)S(1)}, u32[]{:S(2)}, u32[]{:S(2)}) collective-permute-start(bf16[2,128,256]{1,2,0:T(8,128)(2,1)S(1)} %pad_maximum_fusion.3), channel_id=1, source_target_pairs={{0,4},{4,0},{8,12},{12,8},{16,20},{20,16},{24,28},{28,24},{1,5},{5... | collective-permute-start | bytes 393224 | tf_op jit(solution)/shard_map/ppermute | solution.py:14
  77.4 0.9 copy-start.7
  82.2 12.0 %collective-permute-start.1 = (bf16[2,256,256]{1,2,0:T(8,128)(2,1)S(1)}, bf16[2,256,256]{1,2,0:T(8,128)(2,1)S(1)}, u32[]{:S(2)}, u32[]{:S(2)}) collective-permute-start(bf16[2,256,256]{1,2,0:T(8,128)(2,1)S(1)} %pad_maximum_fusion.2), channel_id=1, source_target_pairs={{0,8},{4,12},{8,0},{12,4},{16,24},{20,28},{24,16},{28,20},{1,9},{5... | collective-permute-start | bytes 786440 | tf_op jit(solution)/shard_map/ppermute | solution.py:14
  82.7 11.6 %copy-start.1 = (f32[4,512,512]{1,2,0:T(8,128)S(1)}, f32[4,512,512]{1,2,0:T(8,128)}, u32[]{:S(2)}) copy-start(f32[4,512,512]{1,2,0:T(8,128)} %get-tuple-element.49) | copy-start | bytes 12582916
  94.2 14.7 %collective-permute-start.2 = (bf16[2,512,256]{1,2,0:T(8,128)(2,1)S(1)}, bf16[2,512,256]{1,2,0:T(8,128)(2,1)S(1)}, u32[]{:S(2)}, u32[]{:S(2)}) collective-permute-start(bf16[2,512,256]{1,2,0:T(8,128)(2,1)S(1)} %pad_maximum_fusion.1), channel_id=1, source_target_pairs={{0,16},{4,20},{8,24},{12,28},{16,0},{20,4},{24,8},{28,12},{1,17},{... | collective-permute-start | bytes 1572872 | tf_op jit(solution)/shard_map/ppermute | solution.py:14
  114.7 8.3 %copy-start.2 = (f32[512,256]{0,1:T(8,128)S(1)}, f32[512,256]{0,1:T(8,128)}, u32[]{:S(2)}) copy-start(f32[512,256]{0,1:T(8,128)} %copy.73) | copy-start | bytes 1572868
  114.7 8.3 %copy-start.3 = (f32[512,256]{0,1:T(8,128)S(1)}, f32[512,256]{0,1:T(8,128)}, u32[]{:S(2)}) copy-start(f32[512,256]{0,1:T(8,128)} %copy.82) | copy-start | bytes 1572868
  114.7 8.3 %copy-start.4 = (f32[512,256]{0,1:T(8,128)S(1)}, f32[512,256]{0,1:T(8,128)}, u32[]{:S(2)}) copy-start(f32[512,256]{0,1:T(8,128)} %copy.86) | copy-start | bytes 1572868
Sparse Core Ops, SparseCore 0:
  126.6 28.7 reduce-scatter.1
where the time goes:
time: 165 us; the launch traced here: 164 us
  blocking collectives  55.6 us (34%)
  waiting for transfers between devices  51.2 us (31%)
  local copies, waits for them, and re-layouts  19.3 us (12%)
  between operations  13.7 us (8%)
  other arithmetic  12.1 us (7%)
  matrix products  8.54 us (5%)
  starting transfers between devices  3.61 us (2%)
    reduce_scatter x1, waiting for transfers between devices, per_device(): lax.psum_scatter(jnp.dot(attention, out_weight, preferred_element_type=jn...  28.9 us
    all_gather x1, blocking collectives, per_device(): lax.all_gather(top_key_local, 'seq', axis=0, tiled=True)  28.2 us
    all_gather x1, blocking collectives, per_device(): lax.all_gather(top_value_local, 'seq', axis=0, tiled=True)  27.4 us
    ppermute x3, waiting for transfers between devices, partner_2(): return lax.ppermute(value, axis, pairs)  22.2 us
    select_n x12, local copies, waits for them, and re-layouts, scatter_rows(): spread_out = jnp.where(chosen[None], values[:, None], filler)  12.2 us
    reduce_sum x3, other arithmetic, attend_segment(): total = jnp.sum(mass, axis=2)  4.04 us
    another operation x3, local copies, waits for them, and re-layouts, picked_rows(): block_rows.reshape(group_count, stride, block_rows.shape[1], block_rows.s...  3.82 us
    dot_general x3, matrix products, attend_segment(): jnp.einsum('qhd,khd->hqk', query_matrix_rows, key_matrix_rows, preferred_...  3.67 us
  transfers between devices with their start and end apart: 4, of which 3 were waited for; matrix products, arithmetic and copies ran while one was open for 8% of the time, Pallas kernels for 0%

commit v1 on v0

--- a/solution.py
+++ b/solution.py
@@ -95,6 +95,33 @@
 
 
 def per_device(query, key, value, middle_offsets, upper_offsets, out_weight):
+
+    def load_links(frame_in):
+        arr_now = lax.axis_size("seq")
+        extra = lax.axis_index("seq")
+        u1, work_now, later = (arr_now, extra, frame_in.shape[0])
+        sides = []
+        for rr in range(u1):
+            sides.append((rr, (rr + 1) % u1))
+        nodes = []
+        for rr in range(u1):
+            nodes.append((rr, (rr - 1) % u1))
+        m_next = jnp.zeros((*frame_in.shape[:0], u1 * later, *frame_in.shape[1:]), frame_in.dtype)
+        m_next = lax.dynamic_update_slice_in_dim(m_next, frame_in, work_now * later, axis=0)
+        arr_out = local_part = frame_in
+        f_now = u1 // 2
+        for p in range(1, f_now + 1):
+            arr_out = lax.ppermute(arr_out, axis_name="seq", perm=sides)
+            m_next = lax.dynamic_update_slice_in_dim(
+                m_next, arr_out, (work_now - p) % u1 * later, axis=0
+            )
+            if p < u1 - f_now:
+                local_part = lax.ppermute(local_part, axis_name="seq", perm=nodes)
+                m_next = lax.dynamic_update_slice_in_dim(
+                    m_next, local_part, (work_now + p) % u1 * later, axis=0
+                )
+        return m_next
+
     row_count = query.shape[0]
     head_count = query.shape[1] // HD
     top_stride = lax.axis_size("seq") // 2
@@ -108,7 +135,7 @@
         -1, head_count * HD
     )
     top_key_all, top_value_all = (
-        lax.all_gather(top_key_local, "seq", axis=0, tiled=True),
+        load_links(top_key_local),
         lax.all_gather(top_value_local, "seq", axis=0, tiled=True),
     )
     upper_level = attend_segment(

time: 165 us -> 155 us (0.939)
  blocking collectives: 55.6 us -> 28.7 us
  starting transfers between devices: 3.61 us -> 15.7 us
  local copies, waits for them, and re-layouts: 19.3 us -> 23.4 us
  waiting for transfers between devices: 51.2 us -> 47.3 us
  other arithmetic: 12.1 us -> 15.8 us
    all_gather x1 -> x0, blocking collectives: 28.2 us -> none  [per_device(): lax.all_gather(top_key_local, 'seq', axis=0, tiled=True)]
    ppermute x3, waiting for transfers between devices: 22.2 us -> 5.3 us  [partner_2(): return lax.ppermute(value, axis, pairs)]
    ppermute x0 -> x7, starting transfers between devices: none -> 15.6 us  [the longest x3 12.1 us: load_links(): local_part = lax.ppermute(local_part, axis_name='seq', perm=nodes)]
    ppermute x0 -> x7, waiting for transfers between devices: none -> 11.9 us  [the longest x4 11.9 us: load_links(): arr_out = lax.ppermute(arr_out, axis_name='seq', perm=sides)]
    concatenate x3, other arithmetic: 0.21 us -> 3.74 us  [per_device(): middle_pair = jnp.concatenate([middle_pair, partner], axis=1)]
    ppermute x3, starting transfers between devices: 3.6 us -> 0.08 us  [partner_2(): return lax.ppermute(value, axis, pairs)]
    broadcast_in_dim x6, local copies, waits for them, and re-layouts: 0.57 us -> 3.03 us  [scatter_rows(): spread_out = jnp.where(chosen[None], values[:, None], filler)]
    reduce_sum x3, other arithmetic: 4.04 us -> 1.67 us  [attend_segment(): total = jnp.sum(mass, axis=2)]
  transfers between devices with their start and end apart: 4 -> 11, of which waited for: 3 -> 5; matrix products, arithmetic and copies ran while one was open for 8% -> 12% of each run, Pallas kernels for 0% -> 0%
where the time goes in v1:
time: 155 us; the launch traced here: 154 us
  waiting for transfers between devices  47.3 us (31%)
  blocking collectives  28.7 us (19%)
  local copies, waits for them, and re-layouts  23.4 us (15%)
  other arithmetic  15.8 us (10%)
  starting transfers between devices  15.7 us (10%)
  between operations  14 us (9%)
  matrix products  9.22 us (6%)
    reduce_scatter x1, waiting for transfers between devices, per_device(): lax.psum_scatter(jnp.dot(attention, out_weight, preferred_element_type=jn...  30.1 us
    all_gather x1, blocking collectives, per_device(): lax.all_gather(top_value_local, 'seq', axis=0, tiled=True)  28.7 us
    select_n x12, local copies, waits for them, and re-layouts, scatter_rows(): spread_out = jnp.where(chosen[None], values[:, None], filler)  12.2 us
    ppermute x3, starting transfers between devices, load_links(): local_part = lax.ppermute(local_part, axis_name='seq', perm=nodes)  12.1 us
    ppermute x4, waiting for transfers between devices, load_links(): arr_out = lax.ppermute(arr_out, axis_name='seq', perm=sides)  11.9 us
    ppermute x3, waiting for transfers between devices, partner_2(): return lax.ppermute(value, axis, pairs)  5.3 us
    dot_general x3, matrix products, attend_segment(): jnp.einsum('hqk,khd->qhd', soft_weights, value_matrix_rows, preferred_ele...  4.73 us
    another operation x3, local copies, waits for them, and re-layouts, picked_rows(): block_rows.reshape(group_count, stride, block_rows.shape[1], block_rows.s...  3.81 us
  transfers between devices with their start and end apart: 11, of which 5 were waited for; matrix products, arithmetic and copies ran while one was open for 12% of the time, Pallas kernels for 0%

profile of v1, /device:TPU:0, one launch (start us, length us, event | category | flops | bytes accessed | tf_op | source)
XLA Modules:
  0.0 154.2 jit_solution(723842470958949234)
XLA Ops:
  6.5 1.3 reshape_reshape.16
  7.8 1.2 reshape_reshape.17
  9.1 1.3 reshape_reshape.18
  10.4 3.3 %select_reduce_fusion.4 = (bf16[128,4,64]{2,1,0:T(4,128)(2,1)S(1)}, bf16[128,4,64]{2,1,0:T(4,128)(2,1)S(1)}, bf16[128,4,64]{2,1,0:T(4,128)(2,1)S(1)}, bf16[128,4...) fusion(bf16[128,4,4,64]{3,2,1,0:T(4,128)(2,1)S(1)} %reshape_reshape.17, ...), kind=kLoop, calls=%fused_computation.41 | loop fusion | flops 1376256 | bytes 1179680 | tf_op jit(solution)/shard_map/reduce_sum | solution.py:57
  13.8 3.0 %collective-permute-start.3 = (bf16[128,256]{0,1:T(8,128)(2,1)S(1)}, bf16[128,256]{0,1:T(8,128)(2,1)S(1)}, u32[]{:S(2)}, u32[]{:S(2)}) collective-permute-start(bf16[128,256]{0,1:T(8,128)(2,1)S(1)} %bitcast.103), channel_id=1, source_target_pairs={{0,4},{4,8},{8,12},{12,16},{16,20},{20,24},{24,28},{28,0},{1,5},{5... | collective-permute-start | bytes 196616 | tf_op jit(solution)/shard_map/ppermute | solution.py:114
  16.8 3.1 %collective-permute-start.4 = (bf16[128,256]{0,1:T(8,128)(2,1)S(1)}, bf16[128,256]{0,1:T(8,128)(2,1)S(1)}, u32[]{:S(2)}, u32[]{:S(2)}) collective-permute-start(bf16[128,256]{0,1:T(8,128)(2,1)S(1)} %bitcast.104), channel_id=1, source_target_pairs={{0,28},{4,0},{8,4},{12,8},{16,12},{20,16},{24,20},{28,24},{1,29},{... | collective-permute-start | bytes 196616 | tf_op jit(solution)/shard_map/ppermute | solution.py:119
  21.0 0.6 iota_compare_fusion.1
  21.7 28.7 %all_gather.3 = bf16[1024,256]{0,1:T(8,128)(2,1)} all-gather(bf16[128,256]{0,1:T(8,128)(2,1)S(1)} %bitcast.102), channel_id=1, replica_groups=mesh['seq'=8,'head'=4] {'seq'}, dimensions={0}, use_global_device_ids=true | all-gather | bytes 589824 | tf_op jit(solution)/shard_map/all_gather | solution.py:139
  50.6 0.6 iota_compare_fusion
  51.2 0.8 multiply_reduce_fusion
  52.0 0.7 fusion
  52.7 0.8 fusion.2
  53.7 0.5 collective-permute-start.5
  54.2 4.3 %collective-permute-start.6 = (bf16[128,256]{0,1:T(8,128)(2,1)S(1)}, bf16[128,256]{0,1:T(8,128)(2,1)S(1)}, u32[]{:S(2)}, u32[]{:S(2)}) collective-permute-start(bf16[128,256]{0,1:T(8,128)(2,1)S(1)} %collective-permute-done.4), channel_id=1, source_target_pairs={{0,28},{4,0},{8,4},{12,8},{16,12},{20,16},{24,20},{28,24},{1,29},{... | collective-permute-start | bytes 196616 | tf_op jit(solution)/shard_map/ppermute | solution.py:119
  58.5 0.7 pad_maximum_fusion.2
  59.3 2.2 %collective-permute-done.5 = bf16[128,256]{0,1:T(8,128)(2,1)S(1)} collective-permute-done((bf16[128,256]{0,1:T(8,128)(2,1)S(1)}, bf16[128,256]{0,1:T(8,128)(2,1)S(1)}, u32[]{:S(2)}, u32[]{:S(2)}) %collective-permute-start.5) | collective-permute-done | bytes 65568 | tf_op jit(solution)/shard_map/ppermute | solution.py:114
  61.5 4.7 %collective-permute-start.8 = (bf16[128,256]{0,1:T(8,128)(2,1)S(1)}, bf16[128,256]{0,1:T(8,128)(2,1)S(1)}, u32[]{:S(2)}, u32[]{:S(2)}) collective-permute-start(bf16[128,256]{0,1:T(8,128)(2,1)S(1)} %collective-permute-done.6), channel_id=1, source_target_pairs={{0,28},{4,0},{8,4},{12,8},{16,12},{20,16},{24,20},{28,24},{1,29},{... | collective-permute-start | bytes 196616 | tf_op jit(solution)/shard_map/ppermute | solution.py:119
  66.2 2.2 %collective-permute-done.7 = bf16[128,256]{0,1:T(8,128)(2,1)S(1)} collective-permute-done((bf16[128,256]{0,1:T(8,128)(2,1)S(1)}, bf16[128,256]{0,1:T(8,128)(2,1)S(1)}, u32[]{:S(2)}, u32[]{:S(2)}) %collective-permute-start.7) | collective-permute-done | bytes 65568 | tf_op jit(solution)/shard_map/ppermute | solution.py:114
  68.5 7.5 %collective-permute-done.9 = bf16[128,256]{0,1:T(8,128)(2,1)S(1)} collective-permute-done((bf16[128,256]{0,1:T(8,128)(2,1)S(1)}, bf16[128,256]{0,1:T(8,128)(2,1)S(1)}, u32[]{:S(2)}, u32[]{:S(2)}) %collective-permute-start.9) | collective-permute-done | bytes 65568 | tf_op jit(solution)/shard_map/ppermute | solution.py:114
  76.0 1.4 multiply_reduce_fusion.1
  77.4 0.6 copy-done.8
  78.0 0.5 fusion.8
  78.5 0.7 broadcast_in_dim.204
  79.2 1.7 %copy.92 = f32[128,256]{1,0:T(8,128)} copy(f32[128,256]{0,1:T(8,128)} %bitcast.98) | data formatting | bytes 262144 | tf_op jit(solution)/shard_map/jit(_where)/broadcast_in_dim | solution.py:62
  80.8 1.8 %pad_maximum_fusion.1 = bf16[2,512,256]{1,2,0:T(8,128)(2,1)} fusion(bf16[2,256,256]{1,2,0:T(8,128)(2,1)} %collective-permute-done.1, bf16[2,128,256]{1,2,0:T(8,128)(2,1)S(1)} %collective-permute-done, bf16[1,128,256]{1,2,0:T(8,128)(2,1)S(1)} %bitcast.91, bf16[1,128,256]{1,2,0:T(8,128)(2,1)S(1)} %bitcast.87), kind=kLoop, calls=%fused_computation.26 | loop fusion | flops 2097152 | bytes 1048576 | tf_op jit(solution)/shard_map/concatenate | solution.py:154
  82.6 2.3 %fusion.10 = f32[4,64,128]{2,1,0:T(8,128)} fusion(bf16[1024,4,64]{0,2,1:T(8,128)(2,1)} %bitcast.81, f32[4,128,1024]{2,1,0:T(8,128)S(1)} %get-tuple-element.45, f32[4,128]{1,0:T(4,128)} %copy-done.8), kind=kOutput, calls=%fused_computation.15 | convolution fusion | flops 68681728 | bytes 2754560 | tf_op jit(solution)/shard_map/hqk,khd->qhd/dot_general | solution.py:25
  84.9 1.0 copy.88
  85.9 0.7 broadcast_in_dim.192
  86.7 1.2 broadcast_select_fusion.4
  88.1 1.0 copy.80
  89.3 1.0 copy.89
  90.5 1.0 copy.93
  91.5 5.3 %collective-permute-done.2 = bf16[2,512,256]{1,2,0:T(8,128)(2,1)} collective-permute-done((bf16[2,512,256]{1,2,0:T(8,128)(2,1)}, bf16[2,512,256]{1,2,0:T(8,128)(2,1)}, u32[]{:S(2)}, u32[]{:S(2)}) %collective-permute-start.2) | collective-permute-done | bytes 524320 | tf_op jit(solution)/shard_map/ppermute | solution.py:14
  96.8 1.2 pad_maximum_fusion
  98.0 0.9 fusion.36
  98.9 0.5 multiply_reduce_fusion.2
  99.4 0.5 fusion.6
  100.1 1.6 %fusion.12 = f32[4,64,128]{2,1,0:T(8,128)S(1)} fusion(bf16[1024,4,64]{0,2,1:T(8,128)(2,1)} %bitcast.83, f32[4,128,1024]{2,1,0:T(8,128)S(1)} %get-tuple-element.47, f32[4,128]{1,0:T(4,128)} %copy-done.9), kind=kOutput, calls=%fused_computation.16 | convolution fusion | flops 68681728 | bytes 2754560 | tf_op jit(solution)/shard_map/hqk,khd->qhd/dot_general | solution.py:25
  102.0 1.3 broadcast_select_fusion.5
  103.5 0.2 copy.76
  103.7 2.1 %select_n.142 = f32[512,256]{1,0:T(8,128)} reshape(f32[128,4,256]{2,1,0:T(4,128)} %get-tuple-element.39) | data formatting | bytes 1048576 | tf_op jit(solution)/shard_map/jit(_where)/select_n | solution.py:62
  105.9 2.1 %copy.85 = f32[512,256]{0,1:T(8,128)} copy(f32[512,256]{1,0:T(8,128)} %select_n.142) | data formatting | bytes 1048576 | tf_op jit(solution)/shard_map/jit(_where)/select_n | solution.py:62
  107.9 2.0 %select_n.147 = f32[512,256]{1,0:T(8,128)} reshape(f32[128,4,256]{2,1,0:T(4,128)} %get-tuple-element.40) | data formatting | bytes 1048576 | tf_op jit(solution)/shard_map/jit(_where)/select_n | solution.py:62
  109.9 2.0 %copy.91 = f32[512,256]{0,1:T(8,128)} copy(f32[512,256]{1,0:T(8,128)} %select_n.147) | data formatting | bytes 1048576 | tf_op jit(solution)/shard_map/jit(_where)/select_n | solution.py:62
  112.0 1.6 %fusion.28 = bf16[512,256]{0,1:T(8,128)(2,1)S(1)} fusion(f32[512,256]{0,1:T(8,128)S(1)} %copy-done.3, f32[512,256]{0,1:T(8,128)} %copy.91, f32[512,256]{0,1:T(8,128)S(1)} %copy-done.2, f32[512,256]{0,1:T(8,128)S(1)} %copy-done.1, f32[512,256]{0,1:T(8,128)} %copy.85, f32[512,256]{0,1:T(8,128)S(1)} %copy.76, f32[4,512,64]{1,2,0:T(8,128)S(1)} %fusion.2, ...), kind=kLoop, calls=%fused_computation.43 | loop fusion | flops 2228224 | bytes 3948544 | tf_op jit(solution)/shard_map/convert_element_type | solution.py:94
  113.6 1.8 %fusion.37 = f32[512,1024]{1,0:T(8,128)} fusion(bf16[512,256]{0,1:T(8,128)(2,1)S(1)} %fusion.28, bf16[256,1024]{1,0:T(8,128)(2,1)S(1)} %copy-done), kind=kOutput, calls=%fused_computation.72 | convolution fusion | flops 268435456 | bytes 2883584 | tf_op jit(solution)/shard_map/dot_general | solution.py:169
  115.5 30.1 %reduce-scatter.2.cloned.1.call-done = f32[128,1024]{1,0:T(8,128)} async-done(((f32[512,1024]{1,0:T(8,128)}), f32[128,1024]{1,0:T(8,128)}) %reduce-scatter.2.cloned.1.call-update) | async-done | bytes 524304 | tf_op jit(solution)/shard_map/reduce_scatter | solution.py:168
  145.6 1.8 %convert_element_type.16 = bf16[128,1024]{1,0:T(8,128)(2,1)} convert(f32[128,1024]{1,0:T(8,128)} %reduce-scatter.2.cloned.1.call-done) | non-fusion elementwise | flops 131072 | bytes 786432 | tf_op jit(solution)/shard_map/convert_element_type | solution.py:174
  (72 shorter events, 2.8 us)
Async XLA Ops:
  6.5 107.1 %copy-start = (bf16[256,1024]{1,0:T(8,128)(2,1)S(1)}, bf16[256,1024]{1,0:T(8,128)(2,1)}, u32[]{:S(2)}) copy-start(bf16[256,1024]{1,0:T(8,128)(2,1)} %param.11) | copy-start | bytes 1572868
  6.5 3.8 %copy-start.13 = (s32[4]{0:T(128)S(1)}, s32[4]{0:T(128)}, u32[]{:S(2)}) copy-start(s32[4]{0:T(128)} %param.10) | copy-start | bytes 52
  6.5 3.9 %copy-start.12 = (s32[4]{0:T(128)S(1)}, s32[4]{0:T(128)}, u32[]{:S(2)}) copy-start(s32[4]{0:T(128)} %param.9) | copy-start | bytes 52
  6.5 139.1 %reduce-scatter.2.cloned.1.call-start = ((), (), s32[]{:S(2)}) async-start(), calls=%async_computation.1 | async-start | bytes 2621440 | tf_op jit(solution)/shard_map/reduce_scatter | solution.py:168
  9.1 11.3 %copy-start.4 = (bf16[512,256]{1,0:T(8,128)(2,1)S(1)}, bf16[512,256]{1,0:T(8,128)(2,1)}, u32[]{:S(2)}) copy-start(bf16[512,256]{1,0:T(8,128)(2,1)} %param.6) | copy-start | bytes 786436
  10.4 10.2 %copy-start.5 = (bf16[512,256]{1,0:T(8,128)(2,1)S(1)}, bf16[512,256]{1,0:T(8,128)(2,1)}, u32[]{:S(2)}) copy-start(bf16[512,256]{1,0:T(8,128)(2,1)} %param.7) | copy-start | bytes 786436
  10.4 10.3 %copy-start.6 = (bf16[512,256]{1,0:T(8,128)(2,1)S(1)}, bf16[512,256]{1,0:T(8,128)(2,1)}, u32[]{:S(2)}) copy-start(bf16[512,256]{1,0:T(8,128)(2,1)} %param.8) | copy-start | bytes 786436
  13.7 7.9 %copy-start.7 = (bf16[128,4,64]{2,1,0:T(4,128)(2,1)S(1)}, bf16[128,4,64]{2,1,0:T(4,128)(2,1)}, u32[]{:S(2)}) copy-start(bf16[128,4,64]{2,1,0:T(4,128)(2,1)} %get-tuple-element.33) | copy-start | bytes 196612
  13.8 39.9 %collective-permute-start.3 = (bf16[128,256]{0,1:T(8,128)(2,1)S(1)}, bf16[128,256]{0,1:T(8,128)(2,1)S(1)}, u32[]{:S(2)}, u32[]{:S(2)}) collective-permute-start(bf16[128,256]{0,1:T(8,128)(2,1)S(1)} %bitcast.103), channel_id=1, source_target_pairs={{0,4},{4,8},{8,12},{12,16},{16,20},{20,24},{24,28},{28,0},{1,5},{5... | collective-permute-start | bytes 196616 | tf_op jit(solution)/shard_map/ppermute | solution.py:114
  16.8 37.4 %collective-permute-start.4 = (bf16[128,256]{0,1:T(8,128)(2,1)S(1)}, bf16[128,256]{0,1:T(8,128)(2,1)S(1)}, u32[]{:S(2)}, u32[]{:S(2)}) collective-permute-start(bf16[128,256]{0,1:T(8,128)(2,1)S(1)} %bitcast.104), channel_id=1, source_target_pairs={{0,28},{4,0},{8,4},{12,8},{16,12},{20,16},{24,20},{28,24},{1,29},{... | collective-permute-start | bytes 196616 | tf_op jit(solution)/shard_map/ppermute | solution.py:119
  20.2 38.3 %collective-permute-start = (bf16[2,128,256]{1,2,0:T(8,128)(2,1)S(1)}, bf16[2,128,256]{1,2,0:T(8,128)(2,1)S(1)}, u32[]{:S(2)}, u32[]{:S(2)}) collective-permute-start(bf16[2,128,256]{1,2,0:T(8,128)(2,1)S(1)} %pad_maximum_fusion.3), channel_id=1, source_target_pairs={{0,4},{4,0},{8,12},{12,8},{16,20},{20,16},{24,28},{28,24},{1,5},{5... | collective-permute-start | bytes 393224 | tf_op jit(solution)/shard_map/ppermute | solution.py:14
  53.7 7.8 %collective-permute-start.5 = (bf16[128,256]{0,1:T(8,128)(2,1)S(1)}, bf16[128,256]{0,1:T(8,128)(2,1)S(1)}, u32[]{:S(2)}, u32[]{:S(2)}) collective-permute-start(bf16[128,256]{0,1:T(8,128)(2,1)S(1)} %collective-permute-done.3), channel_id=1, source_target_pairs={{0,4},{4,8},{8,12},{12,16},{16,20},{20,24},{24,28},{28,0},{1,5},{5... | collective-permute-start | bytes 196616 | tf_op jit(solution)/shard_map/ppermute | solution.py:114
  54.2 7.3 %collective-permute-start.6 = (bf16[128,256]{0,1:T(8,128)(2,1)S(1)}, bf16[128,256]{0,1:T(8,128)(2,1)S(1)}, u32[]{:S(2)}, u32[]{:S(2)}) collective-permute-start(bf16[128,256]{0,1:T(8,128)(2,1)S(1)} %collective-permute-done.4), channel_id=1, source_target_pairs={{0,28},{4,0},{8,4},{12,8},{16,12},{20,16},{24,20},{28,24},{1,29},{... | collective-permute-start | bytes 196616 | tf_op jit(solution)/shard_map/ppermute | solution.py:119
  59.3 21.6 %collective-permute-start.1 = (bf16[2,256,256]{1,2,0:T(8,128)(2,1)}, bf16[2,256,256]{1,2,0:T(8,128)(2,1)}, u32[]{:S(2)}, u32[]{:S(2)}) collective-permute-start(bf16[2,256,256]{1,2,0:T(8,128)(2,1)} %pad_maximum_fusion.2), channel_id=1, source_target_pairs={{0,8},{4,12},{8,0},{12,4},{16,24},{20,28},{24,16},{28,20},{1,9},{5... | collective-permute-start | bytes 786440 | tf_op jit(solution)/shard_map/ppermute | solution.py:14
  61.5 7.0 %collective-permute-start.7 = (bf16[128,256]{0,1:T(8,128)(2,1)S(1)}, bf16[128,256]{0,1:T(8,128)(2,1)S(1)}, u32[]{:S(2)}, u32[]{:S(2)}) collective-permute-start(bf16[128,256]{0,1:T(8,128)(2,1)S(1)} %collective-permute-done.5), channel_id=1, source_target_pairs={{0,4},{4,8},{8,12},{12,16},{16,20},{20,24},{24,28},{28,0},{1,5},{5... | collective-permute-start | bytes 196616 | tf_op jit(solution)/shard_map/ppermute | solution.py:114
  61.5 7.0 %collective-permute-start.8 = (bf16[128,256]{0,1:T(8,128)(2,1)S(1)}, bf16[128,256]{0,1:T(8,128)(2,1)S(1)}, u32[]{:S(2)}, u32[]{:S(2)}) collective-permute-start(bf16[128,256]{0,1:T(8,128)(2,1)S(1)} %collective-permute-done.6), channel_id=1, source_target_pairs={{0,28},{4,0},{8,4},{12,8},{16,12},{20,16},{24,20},{28,24},{1,29},{... | collective-permute-start | bytes 196616 | tf_op jit(solution)/shard_map/ppermute | solution.py:119
  68.4 7.6 %collective-permute-start.9 = (bf16[128,256]{0,1:T(8,128)(2,1)S(1)}, bf16[128,256]{0,1:T(8,128)(2,1)S(1)}, u32[]{:S(2)}, u32[]{:S(2)}) collective-permute-start(bf16[128,256]{0,1:T(8,128)(2,1)S(1)} %collective-permute-done.7), channel_id=1, source_target_pairs={{0,4},{4,8},{8,12},{12,16},{16,20},{20,24},{24,28},{28,0},{1,5},{5... | collective-permute-start | bytes 196616 | tf_op jit(solution)/shard_map/ppermute | solution.py:114
  77.4 0.6 copy-start.8
  82.6 14.2 %collective-permute-start.2 = (bf16[2,512,256]{1,2,0:T(8,128)(2,1)}, bf16[2,512,256]{1,2,0:T(8,128)(2,1)}, u32[]{:S(2)}, u32[]{:S(2)}) collective-permute-start(bf16[2,512,256]{1,2,0:T(8,128)(2,1)} %pad_maximum_fusion.1), channel_id=1, source_target_pairs={{0,16},{4,20},{8,24},{12,28},{16,0},{20,4},{24,8},{28,12},{1,17},{... | collective-permute-start | bytes 1572872 | tf_op jit(solution)/shard_map/ppermute | solution.py:14
  99.4 0.6 copy-start.9
  99.9 2.1 %copy-start.11 = (pred[4,256]{1,0:T(4,128)(4,1)S(1)}, pred[4,256]{1,0:T(4,128)(4,1)}, u32[]{:S(2)}) copy-start(pred[4,256]{1,0:T(4,128)(4,1)} %iota_compare_fusion.1) | copy-start | bytes 3076
  100.0 1.8 %copy-start.10 = (f32[4,128]{1,0:T(4,128)S(1)}, f32[4,128]{1,0:T(4,128)}, u32[]{:S(2)}) copy-start(f32[4,128]{1,0:T(4,128)} %copy-done.9) | copy-start | bytes 6148
  103.7 8.3 %copy-start.1 = (f32[512,256]{0,1:T(8,128)S(1)}, f32[512,256]{0,1:T(8,128)}, u32[]{:S(2)}) copy-start(f32[512,256]{0,1:T(8,128)} %copy.80) | copy-start | bytes 1572868
  103.7 8.3 %copy-start.2 = (f32[512,256]{0,1:T(8,128)S(1)}, f32[512,256]{0,1:T(8,128)}, u32[]{:S(2)}) copy-start(f32[512,256]{0,1:T(8,128)} %copy.89) | copy-start | bytes 1572868
  103.7 8.3 %copy-start.3 = (f32[512,256]{0,1:T(8,128)S(1)}, f32[512,256]{0,1:T(8,128)}, u32[]{:S(2)}) copy-start(f32[512,256]{0,1:T(8,128)} %copy.93) | copy-start | bytes 1572868
Sparse Core Ops, SparseCore 0:
  115.6 29.9 reduce-scatter.1
